TPU v7x, 256 devices: a whole 4x4x8 slice. The times are simulated.
256 devices in a mesh: px: 32 (over z_lo, y, x), py: 8 (over z_hi, core).
Axes of the slice: x: 4, y: 4, z: 8 (z_hi: 4, z_lo: 2; z = z_hi * 2 + z_lo), core: 2. Of those that a mesh axis runs over, the one named last changes fastest.
Arguments:
- log_source: float32 [256, 256, 256], P('px', 'py'), may hold values from -12 to 240, as said below
- log_target: float32 [256, 256, 256], P('px', 'py'), may hold values from -12 to 240, as said below
Outputs:
- potential_f: float32 [256, 256, 256], P('px', 'py')
- potential_g: float32 [256, 256, 256], P('px', 'py')
Inputs may be any that keep to these rules, and one draw needn't show every extreme that they name: `log_source`: Log-density values on every cell. `log_target`: Log-density values on every cell.
All inputs are finite; a program needn't handle non-finite values.
Results may differ from a plain program's by a relative error of at most 0.0001.
Values sent between devices are 32-bit elements; how exact they have to be, the bound alone decides.
A program may use at most 128 MiB of HBM per device.

v0:
```python
from functools import partial
import math
import jax
import jax.numpy as jnp
from jax import lax
from jax.sharding import PartitionSpec as P

LEVELS = 3
ITERS = 2
FINE_ITERS = 1
BAND = 16


def epsilon_of(level_index):
    return 0.05 * 2.0 ** (LEVELS - 1 - level_index)


def soft_axis(values, along, level_index):
    inverse_width = 2.0 ** (LEVELS - 1 - level_index) / 18.0
    window = [1, 1, 1]
    window[along] = 2 * BAND + 1
    padding = [(0, 0), (0, 0), (0, 0)]
    padding[along] = (BAND, BAND)
    line_max = lax.reduce_window(
        values, -jnp.inf, lax.max, tuple(window), (1, 1, 1), tuple(padding)
    )
    padded = jnp.pad(values, padding, constant_values=-jnp.inf)
    length = values.shape[along]
    summed = jnp.zeros_like(values)
    for offset in range(2 * BAND + 1):
        shifted = lax.slice_in_dim(padded, offset, offset + length, axis=along)
        weight = math.exp(-float((offset - BAND) ** 2) * inverse_width)
        summed = summed + weight * jnp.exp(shifted - line_max)
    return line_max + jnp.log(summed)


def restrict(values):
    size_a, size_b, size_c = values.shape
    blocks = values.reshape(size_a // 2, 2, size_b // 2, 2, size_c // 2, 2)
    block_max = jnp.max(blocks, axis=(1, 3, 5), keepdims=True)
    merged = block_max + jnp.log(
        jnp.mean(jnp.exp(blocks - block_max), axis=(1, 3, 5), keepdims=True)
    )
    return merged.reshape(size_a // 2, size_b // 2, size_c // 2)


def prolong(values):
    return jnp.repeat(jnp.repeat(jnp.repeat(values, 2, axis=0), 2, axis=1), 2, axis=2)


def unchanged(values):
    return values


def forward(values, rows_fn, columns_fn):
    middle = rows_fn(lax.all_to_all(values, "py", split_axis=2, concat_axis=1, tiled=True))
    return columns_fn(lax.all_to_all(middle, "px", split_axis=1, concat_axis=0, tiled=True))


def backward(values, rows_fn, depth_fn):
    middle = rows_fn(lax.all_to_all(values, "px", split_axis=0, concat_axis=1, tiled=True))
    return depth_fn(lax.all_to_all(middle, "py", split_axis=1, concat_axis=2, tiled=True))


def pencil_level(level_index, source_level, target_level, potential_g):
    epsilon = epsilon_of(level_index)
    sweeps = FINE_ITERS if level_index == LEVELS - 1 else ITERS
    along_first = partial(soft_axis, along=0, level_index=level_index)
    along_second = partial(soft_axis, along=1, level_index=level_index)
    along_third = partial(soft_axis, along=2, level_index=level_index)
    potential_f = potential_g
    source_turned = forward(source_level, unchanged, unchanged)
    turned_f = source_turned
    for iteration in range(sweeps):
        reached = forward(along_third(potential_g / epsilon), along_second, along_first)
        turned_f = epsilon * (source_turned - reached)
        pulled = backward(along_first(turned_f / epsilon), along_second, along_third)
        potential_g = epsilon * (target_level - pulled)
    if level_index == LEVELS - 1:
        potential_f = backward(turned_f, unchanged, unchanged)
    return (potential_f, potential_g)


def per_device(log_source, log_target):
    sources = [log_source]
    targets = [log_target]
    for level_index in range(LEVELS - 1):
        sources = sources + [restrict(sources[-1])]
        targets = targets + [restrict(targets[-1])]
    sources = sources[::-1]
    targets = targets[::-1]
    potential_g = jnp.zeros_like(sources[0])
    potential_f = potential_g
    first_level = 0
    for level_index in range(first_level, LEVELS):
        potential_f, potential_g = pencil_level(
            level_index, sources[level_index], targets[level_index], potential_g
        )
        if level_index < LEVELS - 1:
            potential_g = prolong(potential_g)
    return (potential_f, potential_g)


def solution(mesh):
    return jax.shard_map(
        per_device,
        mesh=mesh,
        in_specs=(P("px", "py", None), P("px", "py", None)),
        out_specs=(P("px", "py", None), P("px", "py", None)),
        check_vma=False,
    )
```

profile of v0, /device:TPU:1, one launch (start us, length us, event | category | flops | bytes accessed | tf_op | source)
XLA Modules:
  0.0 639.6 jit_solution(10024164577190180262)
XLA Ops:
  0.6 18.9 %reshape.69 = f32[4,2,16,2,128,2]{5,4,3,2,1,0:T(8,128)} reshape(f32[8,32,256]{2,1,0:T(8,128)} %param.2) | data formatting | bytes 524288 | tf_op jit(solution)/shard_map/reshape | solution.py:39
  19.5 7.0 %reduce_max.37 = f32[4,16,128]{2,1,0:T(8,128)S(1)} reduce(f32[4,2,16,2,128,2]{5,4,3,2,1,0:T(8,128)} %reshape.69, f32[]{:T(128)} %constant.46.clone.1), dimensions={1,3,5}, to_apply=%region_2.0 | reduce | flops 57344 | bytes 294916 | tf_op jit(solution)/shard_map/reduce_max | solution.py:40
  26.5 8.2 %exponential_reduce_fusion = f32[4,16,128]{2,1,0:T(8,128)S(1)} fusion(f32[4,2,16,2,128,2]{5,4,3,2,1,0:T(8,128)} %reshape.69, f32[4,16,128]{2,1,0:T(8,128)S(1)} %reduce_max.37), kind=kLoop, calls=%fused_computation | loop fusion | flops 122880 | bytes 327680 | tf_op jit(solution)/shard_map/reduce_sum | solution.py:42
  38.5 10.0 %all-to-all-start.4 = ((f32[8,1,128]{2,1,0:T(1,128)}), f32[8,1,128]{2,1,0:T(1,128)S(1)}, u32[]{:S(2)}, u32[]{:S(2)}) async-start(f32[8,1,128]{2,1,0:T(1,128)} %reshape.78), calls=%async_computation.4 | async-start | bytes 8192 | tf_op jit(solution)/shard_map/all_to_all | solution.py:56
  49.5 5.9 all-to-all-done.4
  55.4 3.9 all-to-all-start.6
  59.3 18.1 %reshape.68 = f32[4,2,16,2,128,2]{5,4,3,2,1,0:T(8,128)} reshape(f32[8,32,256]{2,1,0:T(8,128)S(1)} %copy-done.1) | data formatting | bytes 524288 | tf_op jit(solution)/shard_map/reshape | solution.py:39
  77.4 7.0 %reduce_max.36 = f32[4,16,128]{2,1,0:T(8,128)S(1)} reduce(f32[4,2,16,2,128,2]{5,4,3,2,1,0:T(8,128)} %reshape.68, f32[]{:T(128)} %constant.46.clone.1), dimensions={1,3,5}, to_apply=%region_0.0 | reduce | flops 57344 | bytes 294916 | tf_op jit(solution)/shard_map/reduce_max | solution.py:40
  86.4 7.5 %all-to-all-start.5 = ((f32[2,64,8]{2,0,1:T(2,128)}), f32[2,64,8]{2,0,1:T(2,128)S(1)}, u32[]{:S(2)}, u32[]{:S(2)}) async-start(f32[2,64,8]{2,0,1:T(2,128)} %bitcast.15), calls=%async_computation.5 | async-start | bytes 131072 | tf_op jit(solution)/shard_map/all_to_all | solution.py:57
  96.3 5.0 all-to-all-done.5
  101.3 4.1 all-to-all-start.7
  105.4 8.2 %exponential_reduce_fusion.1 = f32[4,16,128]{2,1,0:T(8,128)S(1)} fusion(f32[4,2,16,2,128,2]{5,4,3,2,1,0:T(8,128)} %reshape.68, f32[4,16,128]{2,1,0:T(8,128)S(1)} %reduce_max.36), kind=kLoop, calls=%fused_computation.1 | loop fusion | flops 122880 | bytes 327680 | tf_op jit(solution)/shard_map/reduce_sum | solution.py:42
  113.9 3.5 bitcast_subtract_fusion.4
  117.6 4.0 log_add_fusion.10
  121.6 7.9 %all-to-all-start.8 = ((f32[64,2,8]{2,1,0:T(2,128)}), f32[64,2,8]{2,1,0:T(2,128)S(1)}, u32[]{:S(2)}, u32[]{:S(2)}) async-start(f32[64,2,8]{2,1,0:T(2,128)} %log_add_fusion.10), calls=%async_computation.8 | async-start | bytes 131072 | tf_op jit(solution)/shard_map/all_to_all | solution.py:61
  131.8 4.8 all-to-all-done.8
  138.4 10.1 %all-to-all-start.9 = ((f32[8,1,128]{2,1,0:T(1,128)}), f32[8,1,128]{2,1,0:T(1,128)S(1)}, u32[]{:S(2)}, u32[]{:S(2)}) async-start(f32[8,1,128]{2,1,0:T(1,128)} %reshape.82), calls=%async_computation.9 | async-start | bytes 8192 | tf_op jit(solution)/shard_map/all_to_all | solution.py:62
  149.1 6.3 all-to-all-done.9
  158.2 10.1 %all_to_all.504 = f32[8,1,128]{2,1,0:T(1,128)S(1)} all-to-all(f32[8,1,128]{2,1,0:T(1,128)S(1)} %reshape.84), channel_id=1, replica_groups=mesh['px'=32,'py'=8] {'py'}, dimensions={0} | all-to-all | bytes 8192 | tf_op jit(solution)/shard_map/all_to_all | solution.py:56
  170.1 10.8 %all_to_all.505 = f32[2,64,8]{2,0,1:T(2,128)S(1)} all-to-all(f32[2,64,8]{2,0,1:T(2,128)S(1)} %copy.127), channel_id=1, replica_groups=mesh['px'=32,'py'=8] {'px'}, dimensions={1} | all-to-all | bytes 8192 | tf_op jit(solution)/shard_map/all_to_all | solution.py:57
  181.1 3.5 bitcast_subtract_fusion.3
  184.8 3.4 log_add_fusion.7
  188.2 10.6 %all_to_all.506 = f32[64,2,8]{2,1,0:T(2,128)S(1)} all-to-all(f32[64,2,8]{2,1,0:T(2,128)S(1)} %log_add_fusion.7), channel_id=1, replica_groups=mesh['px'=32,'py'=8] {'px'}, dimensions={0} | all-to-all | bytes 8192 | tf_op jit(solution)/shard_map/all_to_all | solution.py:61
  200.5 6.5 %all-to-all-start.13 = ((f32[8,1,128]{2,1,0:T(1,128)}), f32[8,1,128]{2,1,0:T(1,128)S(1)}, u32[]{:S(2)}, u32[]{:S(2)}) async-start(f32[8,1,128]{2,1,0:T(1,128)} %reshape.86), calls=%async_computation.13 | async-start | bytes 8192 | tf_op jit(solution)/shard_map/all_to_all | solution.py:62
  208.0 6.0 all-to-all-done.13
  214.0 3.9 all-to-all-start.2
  225.1 5.9 all-to-all-start.14
  233.0 5.1 all-to-all-done.14
  238.1 4.0 all-to-all-start.3
  249.3 6.7 %all-to-all-start.15 = ((f32[32,1,256]{2,1,0:T(1,128)}), f32[32,1,256]{2,1,0:T(1,128)S(1)}, u32[]{:S(2)}, u32[]{:S(2)}) async-start(f32[32,1,256]{2,1,0:T(1,128)} %reshape.90), calls=%async_computation.15 | async-start | bytes 65536 | tf_op jit(solution)/shard_map/all_to_all | solution.py:57
  256.9 6.2 all-to-all-done.15
  264.6 6.3 bitcast_subtract_fusion.2
  271.3 6.2 log_add_fusion.5
  277.8 10.7 %all_to_all.507 = f32[32,1,256]{2,1,0:T(1,128)S(1)} all-to-all(f32[32,1,256]{2,1,0:T(1,128)S(1)} %reshape.92), channel_id=1, replica_groups=mesh['px'=32,'py'=8] {'px'}, dimensions={0} | all-to-all | bytes 65536 | tf_op jit(solution)/shard_map/all_to_all | solution.py:61
  293.7 13.1 %all_to_all.508 = f32[8,1,1024]{2,1,0:T(1,128)S(1)} all-to-all(f32[8,1,1024]{2,1,0:T(1,128)S(1)} %reshape.94), channel_id=1, replica_groups=mesh['px'=32,'py'=8] {'py'}, dimensions={0} | all-to-all | bytes 65536 | tf_op jit(solution)/shard_map/all_to_all | solution.py:62
  314.1 10.2 %all_to_all.509 = f32[8,1,1024]{2,1,0:T(1,128)S(1)} all-to-all(f32[8,1,1024]{2,1,0:T(1,128)S(1)} %reshape.96), channel_id=1, replica_groups=mesh['px'=32,'py'=8] {'py'}, dimensions={0} | all-to-all | bytes 65536 | tf_op jit(solution)/shard_map/all_to_all | solution.py:56
  329.7 11.0 %all_to_all.510 = f32[32,1,256]{2,1,0:T(1,128)S(1)} all-to-all(f32[32,1,256]{2,1,0:T(1,128)S(1)} %reshape.98), channel_id=1, replica_groups=mesh['px'=32,'py'=8] {'px'}, dimensions={0} | all-to-all | bytes 65536 | tf_op jit(solution)/shard_map/all_to_all | solution.py:57
  342.0 6.3 bitcast_subtract_fusion.1
  348.8 6.2 log_add_fusion.4
  355.3 10.5 %all_to_all.511 = f32[32,1,256]{2,1,0:T(1,128)S(1)} all-to-all(f32[32,1,256]{2,1,0:T(1,128)S(1)} %reshape.100), channel_id=1, replica_groups=mesh['px'=32,'py'=8] {'px'}, dimensions={0} | all-to-all | bytes 65536 | tf_op jit(solution)/shard_map/all_to_all | solution.py:61
  371.7 6.7 %all-to-all-start.21 = ((f32[8,1,1024]{2,1,0:T(1,128)}), f32[8,1,1024]{2,1,0:T(1,128)S(1)}, u32[]{:S(2)}, u32[]{:S(2)}) async-start(f32[8,1,1024]{2,1,0:T(1,128)} %reshape.102), calls=%async_computation.21 | async-start | bytes 65536 | tf_op jit(solution)/shard_map/all_to_all | solution.py:62
  379.9 5.6 all-to-all-done.21
  385.5 4.2 all-to-all-start
  394.5 9.6 %reduce_window_max.288 = f32[8,32,256]{2,1,0:T(8,128)S(1)} reduce-window(f32[8,32,256]{2,1,0:T(8,128)S(1)} %copy.152, f32[]{:T(128)} %constant.46.clone.1), window={size=1x1x33 pad=0_0x0_0x16_16}, to_apply=%region_31.32 | reduce-window | flops 2097152 | bytes 524292 | tf_op jit(solution)/shard_map/reduce_window_max | solution.py:24
  408.1 7.2 %all-to-all-start.22 = ((f32[8,1,8192]{2,1,0:T(1,128)}), f32[8,1,8192]{2,1,0:T(1,128)S(1)}, u32[]{:S(2)}, u32[]{:S(2)}) async-start(f32[8,1,8192]{2,1,0:T(1,128)} %reshape.104), calls=%async_computation.22 | async-start | bytes 524288 | tf_op jit(solution)/shard_map/all_to_all | solution.py:56
  418.4 7.0 %all-to-all-done.22 = f32[8,1,8192]{2,1,0:T(1,128)S(1)} async-done(((f32[8,1,8192]{2,1,0:T(1,128)}), f32[8,1,8192]{2,1,0:T(1,128)S(1)}, u32[]{:S(2)}, u32[]{:S(2)}) %all-to-all-start.22) | async-done | bytes 262176 | tf_op jit(solution)/shard_map/all_to_all | solution.py:56
  425.4 3.9 all-to-all-start.1
  431.3 18.9 %fusion.2788 = f32[8,256,32]{2,0,1:T(8,128)S(1)} fusion(f32[8,256,32]{2,0,1:T(8,128)S(1)} %bitcast.225), kind=kOutput, calls=%fused_computation.3558 | output fusion | flops 2097152 | bytes 524288 | tf_op jit(solution)/shard_map/reduce_window_max | solution.py:24
  450.1 11.8 %fusion.2778 = f32[256,8,32]{2,1,0:T(8,128)S(1)} fusion(f32[8,256,32]{2,0,1:T(8,128)S(1)} %fusion.2788, f32[8,256,32]{2,0,1:T(8,128)S(1)} %bitcast.226), kind=kLoop, calls=%fused_computation.3541 | loop fusion | flops 6422528 | bytes 786432
  463.1 7.8 %all-to-all-start.23 = ((f32[32,1,2048]{2,1,0:T(1,128)}), f32[32,1,2048]{2,1,0:T(1,128)S(1)}, u32[]{:S(2)}, u32[]{:S(2)}) async-start(f32[32,1,2048]{2,1,0:T(1,128)} %reshape.106), calls=%async_computation.23 | async-start | bytes 524288 | tf_op jit(solution)/shard_map/all_to_all | solution.py:57
  472.6 6.2 all-to-all-done.23
  480.5 18.9 %fusion.2789 = f32[256,8,32]{2,1,0:T(8,128)S(1)} fusion(f32[256,8,32]{2,1,0:T(8,128)S(1)} %bitcast.209), kind=kOutput, calls=%fused_computation.3559 | output fusion | flops 2097152 | bytes 524288 | tf_op jit(solution)/shard_map/reduce_window_max | solution.py:24
  499.4 11.9 %broadcast_multiply_fusion = (f32[256,8,32]{2,1,0:T(8,128)S(1)}, f32[256,8,32]{2,1,0:T(8,128)S(1)}) fusion(f32[256,8,32]{2,1,0:T(8,128)S(1)} %fusion.2789, f32[256,8,32]{2,1,0:T(8,128)S(1)} %bitcast.210, f32[32,8,8,32]{3,2,1,0:T(8,128)S(1)} %copy.107), kind=kLoop, calls=%fused_computation.802 | loop fusion | flops 6553600 | bytes 1310720 | tf_op jit(solution)/shard_map/mul | solution.py:76
  512.5 3.9 all-to-all-start.24
  516.4 18.9 %fusion.2790 = f32[256,8,32]{2,1,0:T(8,128)S(1)} fusion(f32[256,8,32]{2,1,0:T(8,128)S(1)} %get-tuple-element.3), kind=kOutput, calls=%fused_computation.3560 | output fusion | flops 2097152 | bytes 524288 | tf_op jit(solution)/shard_map/reduce_window_max | solution.py:24
  535.2 11.8 %log_add_fusion.1 = f32[256,8,32]{2,1,0:T(8,128)S(1)} fusion(f32[256,8,32]{2,1,0:T(8,128)S(1)} %fusion.2790, f32[256,8,32]{2,1,0:T(8,128)S(1)} %get-tuple-element.3), kind=kLoop, calls=%fused_computation.222 | loop fusion | flops 6422528 | bytes 786432 | tf_op jit(solution)/shard_map/add | solution.py:34
  548.2 7.8 %all-to-all-start.26 = ((f32[32,1,2048]{2,1,0:T(1,128)}), f32[32,1,2048]{2,1,0:T(1,128)S(1)}, u32[]{:S(2)}, u32[]{:S(2)}) async-start(f32[32,1,2048]{2,1,0:T(1,128)} %reshape.112), calls=%async_computation.26 | async-start | bytes 524288 | tf_op jit(solution)/shard_map/all_to_all | solution.py:61
  559.3 4.5 all-to-all-done.26
  563.8 9.3 %all-to-all-start.25 = ((f32[8,1,8192]{2,1,0:T(1,128)}), f32[8,1,8192]{2,1,0:T(1,128)S(1)}, u32[]{:S(2)}, u32[]{:S(2)}) async-start(f32[8,1,8192]{2,1,0:T(1,128)} %reshape.110), calls=%async_computation.25 | async-start | bytes 524288 | tf_op jit(solution)/shard_map/all_to_all | solution.py:62
  574.9 18.9 %fusion.2791 = f32[8,256,32]{2,0,1:T(8,128)S(1)} fusion(f32[8,256,32]{2,0,1:T(8,128)S(1)} %bitcast.227), kind=kOutput, calls=%fused_computation.3561 | output fusion | flops 2097152 | bytes 524288 | tf_op jit(solution)/shard_map/reduce_window_max | solution.py:24
  593.8 11.8 %fusion.2779 = f32[256,8,32]{2,1,0:T(8,128)S(1)} fusion(f32[8,256,32]{2,0,1:T(8,128)S(1)} %fusion.2791, f32[8,256,32]{2,0,1:T(8,128)S(1)} %bitcast.228), kind=kLoop, calls=%fused_computation.3542 | loop fusion | flops 6422528 | bytes 786432
  606.7 7.2 %all-to-all-start.27 = ((f32[8,1,8192]{2,1,0:T(1,128)}), f32[8,1,8192]{2,1,0:T(1,128)S(1)}, u32[]{:S(2)}, u32[]{:S(2)}) async-start(f32[8,1,8192]{2,1,0:T(1,128)} %reshape.114), calls=%async_computation.27 | async-start | bytes 524288 | tf_op jit(solution)/shard_map/all_to_all | solution.py:62
  617.1 6.9 %all-to-all-done.27 = f32[8,1,8192]{2,1,0:T(1,128)S(1)} async-done(((f32[8,1,8192]{2,1,0:T(1,128)}), f32[8,1,8192]{2,1,0:T(1,128)S(1)}, u32[]{:S(2)}, u32[]{:S(2)}) %all-to-all-start.27) | async-done | bytes 262176 | tf_op jit(solution)/shard_map/all_to_all | solution.py:62
  626.5 9.6 %reduce_window_max.293 = f32[8,32,256]{2,1,0:T(8,128)S(1)} reduce-window(f32[8,32,256]{2,1,0:T(8,128)S(1)} %all_to_all.475, f32[]{:T(128)} %constant.46.clone.1), window={size=1x1x33 pad=0_0x0_0x16_16}, to_apply=%region_36.37 | reduce-window | flops 2097152 | bytes 524292 | tf_op jit(solution)/shard_map/reduce_window_max | solution.py:24
  (199 shorter events, 103.5 us)
Async XLA Ops:
  36.8 22.5 %copy-start.1 = (f32[8,32,256]{2,1,0:T(8,128)S(1)}, f32[8,32,256]{2,1,0:T(8,128)}, u32[]{:S(2)}) copy-start(f32[8,32,256]{2,1,0:T(8,128)} %param.3) | copy-start | bytes 786436
  38.5 16.9 %all-to-all-start.4 = ((f32[8,1,128]{2,1,0:T(1,128)}), f32[8,1,128]{2,1,0:T(1,128)S(1)}, u32[]{:S(2)}, u32[]{:S(2)}) async-start(f32[8,1,128]{2,1,0:T(1,128)} %reshape.78), calls=%async_computation.4 | async-start | bytes 8192 | tf_op jit(solution)/shard_map/all_to_all | solution.py:56
  55.4 31.0 %all-to-all-start.6 = ((f32[8,1,128]{2,1,0:T(1,128)}), f32[8,1,128]{2,1,0:T(1,128)S(1)}, u32[]{:S(2)}, u32[]{:S(2)}) async-start(f32[8,1,128]{2,1,0:T(1,128)} %reshape.80), calls=%async_computation.6 | async-start | bytes 8192 | tf_op jit(solution)/shard_map/all_to_all | solution.py:56
  86.4 14.9 %all-to-all-start.5 = ((f32[2,64,8]{2,0,1:T(2,128)}), f32[2,64,8]{2,0,1:T(2,128)S(1)}, u32[]{:S(2)}, u32[]{:S(2)}) async-start(f32[2,64,8]{2,0,1:T(2,128)} %bitcast.15), calls=%async_computation.5 | async-start | bytes 131072 | tf_op jit(solution)/shard_map/all_to_all | solution.py:57
  101.3 12.3 %all-to-all-start.7 = ((f32[2,64,8]{2,0,1:T(2,128)}), f32[2,64,8]{2,0,1:T(2,128)S(1)}, u32[]{:S(2)}, u32[]{:S(2)}) async-start(f32[2,64,8]{2,0,1:T(2,128)} %copy.120), calls=%async_computation.7 | async-start | bytes 131072 | tf_op jit(solution)/shard_map/all_to_all | solution.py:57
  121.6 15.1 %all-to-all-start.8 = ((f32[64,2,8]{2,1,0:T(2,128)}), f32[64,2,8]{2,1,0:T(2,128)S(1)}, u32[]{:S(2)}, u32[]{:S(2)}) async-start(f32[64,2,8]{2,1,0:T(2,128)} %log_add_fusion.10), calls=%async_computation.8 | async-start | bytes 131072 | tf_op jit(solution)/shard_map/all_to_all | solution.py:61
  138.4 17.1 %all-to-all-start.9 = ((f32[8,1,128]{2,1,0:T(1,128)}), f32[8,1,128]{2,1,0:T(1,128)S(1)}, u32[]{:S(2)}, u32[]{:S(2)}) async-start(f32[8,1,128]{2,1,0:T(1,128)} %reshape.82), calls=%async_computation.9 | async-start | bytes 8192 | tf_op jit(solution)/shard_map/all_to_all | solution.py:62
  200.5 13.4 %all-to-all-start.13 = ((f32[8,1,128]{2,1,0:T(1,128)}), f32[8,1,128]{2,1,0:T(1,128)S(1)}, u32[]{:S(2)}, u32[]{:S(2)}) async-start(f32[8,1,128]{2,1,0:T(1,128)} %reshape.86), calls=%async_computation.13 | async-start | bytes 8192 | tf_op jit(solution)/shard_map/all_to_all | solution.py:62
  214.0 11.1 %all-to-all-start.2 = ((f32[8,1,1024]{2,1,0:T(1,128)}), f32[8,1,1024]{2,1,0:T(1,128)S(1)}, u32[]{:S(2)}, u32[]{:S(2)}) async-start(f32[8,1,1024]{2,1,0:T(1,128)} %reshape.74), calls=%async_computation.2 | async-start | bytes 65536 | tf_op jit(solution)/shard_map/all_to_all | solution.py:56
  225.1 13.0 %all-to-all-start.14 = ((f32[8,1,1024]{2,1,0:T(1,128)}), f32[8,1,1024]{2,1,0:T(1,128)S(1)}, u32[]{:S(2)}, u32[]{:S(2)}) async-start(f32[8,1,1024]{2,1,0:T(1,128)} %reshape.88), calls=%async_computation.14 | async-start | bytes 65536 | tf_op jit(solution)/shard_map/all_to_all | solution.py:56
  238.1 11.2 %all-to-all-start.3 = ((f32[32,1,256]{2,1,0:T(1,128)}), f32[32,1,256]{2,1,0:T(1,128)S(1)}, u32[]{:S(2)}, u32[]{:S(2)}) async-start(f32[32,1,256]{2,1,0:T(1,128)} %reshape.76), calls=%async_computation.3 | async-start | bytes 65536 | tf_op jit(solution)/shard_map/all_to_all | solution.py:57
  249.3 13.9 %all-to-all-start.15 = ((f32[32,1,256]{2,1,0:T(1,128)}), f32[32,1,256]{2,1,0:T(1,128)S(1)}, u32[]{:S(2)}, u32[]{:S(2)}) async-start(f32[32,1,256]{2,1,0:T(1,128)} %reshape.90), calls=%async_computation.15 | async-start | bytes 65536 | tf_op jit(solution)/shard_map/all_to_all | solution.py:57
  348.8 29.5 %copy-start = (f32[8,32,256]{2,1,0:T(8,128)S(1)}, f32[8,32,256]{2,1,0:T(8,128)}, u32[]{:S(2)}) copy-start(f32[8,32,256]{2,1,0:T(8,128)} %param.2) | copy-start | bytes 786436
  371.7 13.8 %all-to-all-start.21 = ((f32[8,1,1024]{2,1,0:T(1,128)}), f32[8,1,1024]{2,1,0:T(1,128)S(1)}, u32[]{:S(2)}, u32[]{:S(2)}) async-start(f32[8,1,1024]{2,1,0:T(1,128)} %reshape.102), calls=%async_computation.21 | async-start | bytes 65536 | tf_op jit(solution)/shard_map/all_to_all | solution.py:62
  385.5 22.6 %all-to-all-start = ((f32[8,1,8192]{2,1,0:T(1,128)}), f32[8,1,8192]{2,1,0:T(1,128)S(1)}, u32[]{:S(2)}, u32[]{:S(2)}) async-start(f32[8,1,8192]{2,1,0:T(1,128)} %reshape.70), calls=%async_computation | async-start | bytes 524288 | tf_op jit(solution)/shard_map/all_to_all | solution.py:56
  408.1 17.3 %all-to-all-start.22 = ((f32[8,1,8192]{2,1,0:T(1,128)}), f32[8,1,8192]{2,1,0:T(1,128)S(1)}, u32[]{:S(2)}, u32[]{:S(2)}) async-start(f32[8,1,8192]{2,1,0:T(1,128)} %reshape.104), calls=%async_computation.22 | async-start | bytes 524288 | tf_op jit(solution)/shard_map/all_to_all | solution.py:56
  425.4 37.7 %all-to-all-start.1 = ((f32[32,1,2048]{2,1,0:T(1,128)}), f32[32,1,2048]{2,1,0:T(1,128)S(1)}, u32[]{:S(2)}, u32[]{:S(2)}) async-start(f32[32,1,2048]{2,1,0:T(1,128)} %reshape.72), calls=%async_computation.1 | async-start | bytes 524288 | tf_op jit(solution)/shard_map/all_to_all | solution.py:57
  463.1 15.7 %all-to-all-start.23 = ((f32[32,1,2048]{2,1,0:T(1,128)}), f32[32,1,2048]{2,1,0:T(1,128)S(1)}, u32[]{:S(2)}, u32[]{:S(2)}) async-start(f32[32,1,2048]{2,1,0:T(1,128)} %reshape.106), calls=%async_computation.23 | async-start | bytes 524288 | tf_op jit(solution)/shard_map/all_to_all | solution.py:57
  512.5 35.7 %all-to-all-start.24 = ((f32[32,1,2048]{2,1,0:T(1,128)}), f32[32,1,2048]{2,1,0:T(1,128)S(1)}, u32[]{:S(2)}, u32[]{:S(2)}) async-start(f32[32,1,2048]{2,1,0:T(1,128)} %reshape.108), calls=%async_computation.24 | async-start | bytes 524288 | tf_op jit(solution)/shard_map/all_to_all | solution.py:61
  548.2 15.7 %all-to-all-start.26 = ((f32[32,1,2048]{2,1,0:T(1,128)}), f32[32,1,2048]{2,1,0:T(1,128)S(1)}, u32[]{:S(2)}, u32[]{:S(2)}) async-start(f32[32,1,2048]{2,1,0:T(1,128)} %reshape.112), calls=%async_computation.26 | async-start | bytes 524288 | tf_op jit(solution)/shard_map/all_to_all | solution.py:61
  563.8 42.9 %all-to-all-start.25 = ((f32[8,1,8192]{2,1,0:T(1,128)}), f32[8,1,8192]{2,1,0:T(1,128)S(1)}, u32[]{:S(2)}, u32[]{:S(2)}) async-start(f32[8,1,8192]{2,1,0:T(1,128)} %reshape.110), calls=%async_computation.25 | async-start | bytes 524288 | tf_op jit(solution)/shard_map/all_to_all | solution.py:62
  606.7 17.3 %all-to-all-start.27 = ((f32[8,1,8192]{2,1,0:T(1,128)}), f32[8,1,8192]{2,1,0:T(1,128)S(1)}, u32[]{:S(2)}, u32[]{:S(2)}) async-start(f32[8,1,8192]{2,1,0:T(1,128)} %reshape.114), calls=%async_computation.27 | async-start | bytes 524288 | tf_op jit(solution)/shard_map/all_to_all | solution.py:62
where the time goes:
time: 650 us; the launch traced here: 640 us
  other arithmetic  273 us (42%)
  starting transfers between devices  128 us (20%)
  blocking collectives  87 us (13%)
  local copies, waits for them, and re-layouts  76.4 us (12%)
  waiting for transfers between devices  72.1 us (11%)
    another operation x29, other arithmetic, soft_axis(): lax.reduce_window(values, -jnp.inf, lax.max, tuple(window), (1, 1, 1), tu...  119 us
    add x17, other arithmetic, soft_axis(): return line_max + jnp.log(summed)  44.7 us
    all_to_all x5, starting transfers between devices, backward(): lax.all_to_all(middle, 'py', split_axis=1, concat_axis=2, tiled=True)  39.8 us
    reshape x2, local copies, waits for them, and re-layouts, restrict(): blocks = values.reshape(size_a // 2, 2, size_b // 2, 2, size_c // 2, 2)  36.9 us
    all_to_all x6, starting transfers between devices, forward(): lax.all_to_all(values, 'py', split_axis=2, concat_axis=1, tiled=True)  35.2 us
    all_to_all x6, starting transfers between devices, forward(): lax.all_to_all(middle, 'px', split_axis=1, concat_axis=0, tiled=True)  33.9 us
    all_to_all x3, blocking collectives, backward(): lax.all_to_all(values, 'px', split_axis=0, concat_axis=1, tiled=True)  31.9 us
    all_to_all x5, waiting for transfers between devices, backward(): lax.all_to_all(middle, 'py', split_axis=1, concat_axis=2, tiled=True)  24.8 us
  transfers between devices with their start and end apart: 20, of which 14 were waited for; matrix products, arithmetic and copies ran while one was open for 29% of the time, Pallas kernels for 0%

commit v1 on v0

--- a/solution.py
+++ b/solution.py
@@ -54,7 +54,17 @@
 
 def forward(values, rows_fn, columns_fn):
     middle = rows_fn(lax.all_to_all(values, "py", split_axis=2, concat_axis=1, tiled=True))
-    return columns_fn(lax.all_to_all(middle, "px", split_axis=1, concat_axis=0, tiled=True))
+    return columns_fn(
+        jnp.concatenate(
+            lax.all_to_all(
+                jnp.stack(jnp.split(middle, lax.axis_size("px"), axis=1), axis=0),
+                axis_name="px",
+                split_axis=0,
+                concat_axis=0,
+            ),
+            axis=0,
+        )
+    )
 
 
 def backward(values, rows_fn, depth_fn):

time: 650 us -> 699 us (1.075)
  local copies, waits for them, and re-layouts: 76.4 us -> 118 us
  blocking collectives: 87 us -> 54.9 us
  waiting for transfers between devices: 72.1 us -> 95.9 us
  starting transfers between devices: 128 us -> 139 us
    unnamed x52 -> x304, local copies, waits for them, and re-layouts: 23.7 us -> 64.6 us
    all_to_all x3 -> x1, blocking collectives: 31.9 us -> 10.7 us  [backward(): lax.all_to_all(values, 'px', split_axis=0, concat_axis=1, tiled=True)]
    all_to_all x6 -> x7, waiting for transfers between devices: 18.6 us -> 32.4 us  [forward(): lax.all_to_all(jnp.stack(jnp.split(middle, lax.axis_size('px'), axis=1),...]
    add x17 -> x18, other arithmetic: 44.7 us -> 57.7 us  [soft_axis(): return line_max + jnp.log(summed)]
    unnamed x2 -> x1, other arithmetic: 23.5 us -> 11.8 us
    all_to_all x2 -> x1, blocking collectives: 21.8 us -> 10.8 us  [forward(): lax.all_to_all(jnp.stack(jnp.split(middle, lax.axis_size('px'), axis=1),...]
    all_to_all x3 -> x5, waiting for transfers between devices: 9.37 us -> 20.1 us  [backward(): lax.all_to_all(values, 'px', split_axis=0, concat_axis=1, tiled=True)]
    all_to_all x6 -> x7, starting transfers between devices: 33.9 us -> 38.2 us  [forward(): lax.all_to_all(jnp.stack(jnp.split(middle, lax.axis_size('px'), axis=1),...]
  transfers between devices with their start and end apart: 20 -> 23, of which waited for: 14 -> 17; matrix products, arithmetic and copies ran while one was open for 29% -> 29% of each run, Pallas kernels for 0% -> 0%
where the time goes in v1:
time: 699 us; the launch traced here: 688 us
  other arithmetic  277 us (40%)
  starting transfers between devices  139 us (20%)
  local copies, waits for them, and re-layouts  118 us (17%)
  waiting for transfers between devices  95.9 us (14%)
  blocking collectives  54.9 us (8%)
    another operation x29, other arithmetic, soft_axis(): lax.reduce_window(values, -jnp.inf, lax.max, tuple(window), (1, 1, 1), tu...  119 us
    unnamed x304, local copies, waits for them, and re-layouts  64.6 us
    add x18, other arithmetic, soft_axis(): return line_max + jnp.log(summed)  57.7 us
    all_to_all x5, starting transfers between devices, backward(): lax.all_to_all(middle, 'py', split_axis=1, concat_axis=2, tiled=True)  39.8 us
    all_to_all x7, starting transfers between devices, forward(): lax.all_to_all(jnp.stack(jnp.split(middle, lax.axis_size('px'), axis=1),...  38.2 us
    all_to_all x6, starting transfers between devices, forward(): lax.all_to_all(values, 'py', split_axis=2, concat_axis=1, tiled=True)  37.3 us
    reshape x2, local copies, waits for them, and re-layouts, restrict(): blocks = values.reshape(size_a // 2, 2, size_b // 2, 2, size_c // 2, 2)  36.9 us
    all_to_all x7, waiting for transfers between devices, forward(): lax.all_to_all(jnp.stack(jnp.split(middle, lax.axis_size('px'), axis=1),...  32.4 us
  transfers between devices with their start and end apart: 23, of which 17 were waited for; matrix products, arithmetic and copies ran while one was open for 29% of the time, Pallas kernels for 0%

profile of v1, /device:TPU:1, one launch (start us, length us, event | category | flops | bytes accessed | tf_op | source)
XLA Modules:
  0.0 688.3 jit_solution(9222823978520933384)
XLA Ops:
  0.6 18.9 %reshape.94 = f32[4,2,16,2,128,2]{5,4,3,2,1,0:T(8,128)} reshape(f32[8,32,256]{2,1,0:T(8,128)} %param.2) | data formatting | bytes 524288 | tf_op jit(solution)/shard_map/reshape | solution.py:39
  19.5 7.0 %reduce_max.37 = f32[4,16,128]{2,1,0:T(8,128)S(1)} reduce(f32[4,2,16,2,128,2]{5,4,3,2,1,0:T(8,128)} %reshape.94, f32[]{:T(128)} %constant.46.clone.1), dimensions={1,3,5}, to_apply=%region_2.0 | reduce | flops 57344 | bytes 294916 | tf_op jit(solution)/shard_map/reduce_max | solution.py:40
  26.5 8.2 %exponential_reduce_fusion = f32[4,16,128]{2,1,0:T(8,128)S(1)} fusion(f32[4,2,16,2,128,2]{5,4,3,2,1,0:T(8,128)} %reshape.94, f32[4,16,128]{2,1,0:T(8,128)S(1)} %reduce_max.37), kind=kLoop, calls=%fused_computation | loop fusion | flops 122880 | bytes 327680 | tf_op jit(solution)/shard_map/reduce_sum | solution.py:42
  38.5 10.0 %all-to-all-start.4 = ((f32[8,1,128]{2,1,0:T(1,128)}), f32[8,1,128]{2,1,0:T(1,128)S(1)}, u32[]{:S(2)}, u32[]{:S(2)}) async-start(f32[8,1,128]{2,1,0:T(1,128)} %reshape.110), calls=%async_computation.4 | async-start | bytes 8192 | tf_op jit(solution)/shard_map/all_to_all | solution.py:56
  48.5 18.1 %reshape.93 = f32[4,2,16,2,128,2]{5,4,3,2,1,0:T(8,128)} reshape(f32[8,32,256]{2,1,0:T(8,128)S(1)} %copy-done.3) | data formatting | bytes 524288 | tf_op jit(solution)/shard_map/reshape | solution.py:39
  66.6 7.0 %reduce_max.36 = f32[4,16,128]{2,1,0:T(8,128)S(1)} reduce(f32[4,2,16,2,128,2]{5,4,3,2,1,0:T(8,128)} %reshape.93, f32[]{:T(128)} %constant.46.clone.1), dimensions={1,3,5}, to_apply=%region_0.0 | reduce | flops 57344 | bytes 294916 | tf_op jit(solution)/shard_map/reduce_max | solution.py:40
  73.6 8.2 %exponential_reduce_fusion.1 = f32[4,16,128]{2,1,0:T(8,128)S(1)} fusion(f32[4,2,16,2,128,2]{5,4,3,2,1,0:T(8,128)} %reshape.93, f32[4,16,128]{2,1,0:T(8,128)S(1)} %reduce_max.36), kind=kLoop, calls=%fused_computation.1 | loop fusion | flops 122880 | bytes 327680 | tf_op jit(solution)/shard_map/reduce_sum | solution.py:42
  82.8 7.2 %all-to-all-start.6 = ((f32[8,1,128]{2,1,0:T(1,128)}), f32[8,1,128]{2,1,0:T(1,128)S(1)}, u32[]{:S(2)}, u32[]{:S(2)}) async-start(f32[8,1,128]{2,1,0:T(1,128)} %reshape.112), calls=%async_computation.6 | async-start | bytes 8192 | tf_op jit(solution)/shard_map/all_to_all | solution.py:56
  130.0 7.5 %all-to-all-start.7 = ((f32[32,2,2,8]{3,2,1,0:T(2,128)}), f32[32,2,2,8]{3,2,1,0:T(2,128)S(1)}, u32[]{:S(2)}, u32[]{:S(2)}) async-start(f32[32,2,2,8]{3,2,1,0:T(2,128)} %constant_dynamic-update-slice_fusion.96), calls=%async_computation.7 | async-start | bytes 131072 | tf_op jit(solution)/shard_map/all_to_all | solution.py:59
  138.1 6.7 all-to-all-done.7
  144.8 3.9 all-to-all-start.5
  148.8 7.0 %all-to-all-done.5 = f32[32,2,2,8]{3,2,1,0:T(2,128)S(1)} async-done(((f32[32,2,2,8]{3,2,1,0:T(2,128)}), f32[32,2,2,8]{3,2,1,0:T(2,128)S(1)}, u32[]{:S(2)}, u32[]{:S(2)}) %all-to-all-start.5) | async-done | bytes 4128 | tf_op jit(solution)/shard_map/all_to_all | solution.py:59
  159.4 4.0 log_add_fusion.10
  163.4 3.9 all-to-all-start.8
  169.6 4.8 all-to-all-done.8
  176.2 10.8 %all-to-all-start.9 = ((f32[8,1,128]{2,1,0:T(1,128)}), f32[8,1,128]{2,1,0:T(1,128)S(1)}, u32[]{:S(2)}, u32[]{:S(2)}) async-start(f32[8,1,128]{2,1,0:T(1,128)} %reshape.114), calls=%async_computation.9 | async-start | bytes 8192 | tf_op jit(solution)/shard_map/all_to_all | solution.py:72
  187.7 6.3 all-to-all-done.9
  196.9 10.1 %all_to_all.400 = f32[8,1,128]{2,1,0:T(1,128)S(1)} all-to-all(f32[8,1,128]{2,1,0:T(1,128)S(1)} %reshape.116), channel_id=1, replica_groups=mesh['px'=32,'py'=8] {'py'}, dimensions={0} | all-to-all | bytes 8192 | tf_op jit(solution)/shard_map/all_to_all | solution.py:56
  209.3 10.8 %all_to_all.401 = f32[32,2,2,8]{3,2,1,0:T(2,128)S(1)} all-to-all(f32[32,2,2,8]{3,2,1,0:T(2,128)S(1)} %constant_dynamic-update-slice_fusion.128), channel_id=1, replica_groups=mesh['px'=32,'py'=8] {'px'}, dimensions={0} | all-to-all | bytes 8192 | tf_op jit(solution)/shard_map/all_to_all | solution.py:59
  223.9 4.0 log_add_fusion.7
  227.9 3.9 all-to-all-start.12
  232.7 6.2 all-to-all-done.12
  238.9 6.5 all-to-all-start.2
  247.2 5.4 all-to-all-done.2
  252.6 3.9 all-to-all-start.13
  269.5 3.9 all-to-all-start.14
  275.2 5.4 all-to-all-done.14
  280.6 4.0 all-to-all-start.3
  291.7 7.1 %all-to-all-start.15 = ((f32[32,1,256]{2,1,0:T(1,128)}), f32[32,1,256]{2,1,0:T(1,128)S(1)}, u32[]{:S(2)}, u32[]{:S(2)}) async-start(f32[32,1,256]{2,1,0:T(1,128)} %reshape.122), calls=%async_computation.15 | async-start | bytes 65536 | tf_op jit(solution)/shard_map/all_to_all | solution.py:59
  299.9 6.2 all-to-all-done.15
  307.5 6.3 bitcast_subtract_fusion.2
  314.3 6.2 log_add_fusion.5
  320.7 10.7 %all_to_all.402 = f32[32,1,256]{2,1,0:T(1,128)S(1)} all-to-all(f32[32,1,256]{2,1,0:T(1,128)S(1)} %reshape.124), channel_id=1, replica_groups=mesh['px'=32,'py'=8] {'px'}, dimensions={0} | all-to-all | bytes 65536 | tf_op jit(solution)/shard_map/all_to_all | solution.py:71
  336.8 13.1 %all_to_all.403 = f32[8,1,1024]{2,1,0:T(1,128)S(1)} all-to-all(f32[8,1,1024]{2,1,0:T(1,128)S(1)} %reshape.126), channel_id=1, replica_groups=mesh['px'=32,'py'=8] {'py'}, dimensions={0} | all-to-all | bytes 65536 | tf_op jit(solution)/shard_map/all_to_all | solution.py:72
  357.3 10.2 %all_to_all.404 = f32[8,1,1024]{2,1,0:T(1,128)S(1)} all-to-all(f32[8,1,1024]{2,1,0:T(1,128)S(1)} %reshape.128), channel_id=1, replica_groups=mesh['px'=32,'py'=8] {'py'}, dimensions={0} | all-to-all | bytes 65536 | tf_op jit(solution)/shard_map/all_to_all | solution.py:56
  379.4 5.6 all-to-all-done.19
  384.9 5.7 all-to-all-start
  392.1 6.3 bitcast_subtract_fusion.1
  398.8 6.2 log_add_fusion.4
  405.9 3.9 all-to-all-start.20
  412.2 4.7 all-to-all-done.20
  422.9 8.6 %all-to-all-start.21 = ((f32[8,1,1024]{2,1,0:T(1,128)}), f32[8,1,1024]{2,1,0:T(1,128)S(1)}, u32[]{:S(2)}, u32[]{:S(2)}) async-start(f32[8,1,1024]{2,1,0:T(1,128)} %reshape.134), calls=%async_computation.21 | async-start | bytes 65536 | tf_op jit(solution)/shard_map/all_to_all | solution.py:72
  431.5 7.1 %all-to-all-done.21 = f32[8,1,1024]{2,1,0:T(1,128)S(1)} async-done(((f32[8,1,1024]{2,1,0:T(1,128)}), f32[8,1,1024]{2,1,0:T(1,128)S(1)}, u32[]{:S(2)}, u32[]{:S(2)}) %all-to-all-start.21) | async-done | bytes 32800 | tf_op jit(solution)/shard_map/all_to_all | solution.py:72
  443.5 9.6 %reduce_window_max.288 = f32[8,32,256]{2,1,0:T(8,128)S(1)} reduce-window(f32[8,32,256]{2,1,0:T(8,128)S(1)} %copy.467, f32[]{:T(128)} %constant.46.clone.1), window={size=1x1x33 pad=0_0x0_0x16_16}, to_apply=%region_31.32 | reduce-window | flops 2097152 | bytes 524292 | tf_op jit(solution)/shard_map/reduce_window_max | solution.py:24
  458.8 4.0 all-to-all-start.22
  464.0 9.0 %all-to-all-done.22 = f32[8,1,8192]{2,1,0:T(1,128)S(1)} async-done(((f32[8,1,8192]{2,1,0:T(1,128)}), f32[8,1,8192]{2,1,0:T(1,128)S(1)}, u32[]{:S(2)}, u32[]{:S(2)}) %all-to-all-start.22) | async-done | bytes 262176 | tf_op jit(solution)/shard_map/all_to_all | solution.py:56
  473.1 3.9 all-to-all-start.1
  479.1 18.9 %fusion.2787 = f32[8,256,32]{2,0,1:T(8,128)S(1)} fusion(f32[8,256,32]{2,0,1:T(8,128)S(1)} %bitcast.1243), kind=kOutput, calls=%fused_computation.4066 | output fusion | flops 2097152 | bytes 524288 | tf_op jit(solution)/shard_map/reduce_window_max | solution.py:24
  497.9 11.8 %log_add_fusion.2 = f32[8,256,32]{2,0,1:T(8,128)S(1)} fusion(f32[8,256,32]{2,0,1:T(8,128)S(1)} %fusion.2787, f32[8,256,32]{2,0,1:T(8,128)S(1)} %bitcast.1244), kind=kLoop, calls=%fused_computation.523 | loop fusion | flops 6422528 | bytes 786432 | tf_op jit(solution)/shard_map/add | solution.py:34
  511.3 8.0 %all-to-all-start.23 = ((f32[32,1,2048]{2,1,0:T(1,128)}), f32[32,1,2048]{2,1,0:T(1,128)S(1)}, u32[]{:S(2)}, u32[]{:S(2)}) async-start(f32[32,1,2048]{2,1,0:T(1,128)} %reshape.138), calls=%async_computation.23 | async-start | bytes 524288 | tf_op jit(solution)/shard_map/all_to_all | solution.py:59
  520.9 6.2 all-to-all-done.23
  529.0 18.9 %fusion.2788 = f32[256,8,32]{2,1,0:T(8,128)S(1)} fusion(f32[256,8,32]{2,1,0:T(8,128)S(1)} %bitcast.1197), kind=kOutput, calls=%fused_computation.4067 | output fusion | flops 2097152 | bytes 524288 | tf_op jit(solution)/shard_map/reduce_window_max | solution.py:24
  547.9 11.9 %broadcast_multiply_fusion = (f32[256,8,32]{2,1,0:T(8,128)S(1)}, f32[256,8,32]{2,1,0:T(8,128)S(1)}) fusion(f32[256,8,32]{2,1,0:T(8,128)S(1)} %fusion.2788, f32[256,8,32]{2,1,0:T(8,128)S(1)} %bitcast.1198, f32[32,8,8,32]{3,2,1,0:T(8,128)S(1)} %reshape.105), kind=kLoop, calls=%fused_computation.1058 | loop fusion | flops 6553600 | bytes 1310720 | tf_op jit(solution)/shard_map/mul | solution.py:86
  561.0 3.9 all-to-all-start.24
  564.9 18.9 %fusion.2789 = f32[256,8,32]{2,1,0:T(8,128)S(1)} fusion(f32[256,8,32]{2,1,0:T(8,128)S(1)} %get-tuple-element.3), kind=kOutput, calls=%fused_computation.4068 | output fusion | flops 2097152 | bytes 524288 | tf_op jit(solution)/shard_map/reduce_window_max | solution.py:24
  583.7 11.8 %log_add_fusion.1 = f32[256,8,32]{2,1,0:T(8,128)S(1)} fusion(f32[256,8,32]{2,1,0:T(8,128)S(1)} %fusion.2789, f32[256,8,32]{2,1,0:T(8,128)S(1)} %get-tuple-element.3), kind=kLoop, calls=%fused_computation.222 | loop fusion | flops 6422528 | bytes 786432 | tf_op jit(solution)/shard_map/add | solution.py:34
  596.7 7.8 %all-to-all-start.26 = ((f32[32,1,2048]{2,1,0:T(1,128)}), f32[32,1,2048]{2,1,0:T(1,128)S(1)}, u32[]{:S(2)}, u32[]{:S(2)}) async-start(f32[32,1,2048]{2,1,0:T(1,128)} %reshape.144), calls=%async_computation.26 | async-start | bytes 524288 | tf_op jit(solution)/shard_map/all_to_all | solution.py:71
  608.0 4.4 all-to-all-done.26
  612.3 9.3 %all-to-all-start.25 = ((f32[8,1,8192]{2,1,0:T(1,128)}), f32[8,1,8192]{2,1,0:T(1,128)S(1)}, u32[]{:S(2)}, u32[]{:S(2)}) async-start(f32[8,1,8192]{2,1,0:T(1,128)} %reshape.142), calls=%async_computation.25 | async-start | bytes 524288 | tf_op jit(solution)/shard_map/all_to_all | solution.py:72
  623.5 18.9 %fusion.2790 = f32[8,256,32]{2,0,1:T(8,128)S(1)} fusion(f32[8,256,32]{2,0,1:T(8,128)S(1)} %bitcast.1245), kind=kOutput, calls=%fused_computation.4069 | output fusion | flops 2097152 | bytes 524288 | tf_op jit(solution)/shard_map/reduce_window_max | solution.py:24
  642.4 11.8 %fusion.2778 = f32[256,8,32]{2,1,0:T(8,128)S(1)} fusion(f32[8,256,32]{2,0,1:T(8,128)S(1)} %fusion.2790, f32[8,256,32]{2,0,1:T(8,128)S(1)} %bitcast.1246), kind=kLoop, calls=%fused_computation.4052 | loop fusion | flops 6422528 | bytes 786432
  655.3 7.2 %all-to-all-start.27 = ((f32[8,1,8192]{2,1,0:T(1,128)}), f32[8,1,8192]{2,1,0:T(1,128)S(1)}, u32[]{:S(2)}, u32[]{:S(2)}) async-start(f32[8,1,8192]{2,1,0:T(1,128)} %reshape.146), calls=%async_computation.27 | async-start | bytes 524288 | tf_op jit(solution)/shard_map/all_to_all | solution.py:72
  665.8 6.8 all-to-all-done.27
  675.2 9.6 %reduce_window_max.293 = f32[8,32,256]{2,1,0:T(8,128)S(1)} reduce-window(f32[8,32,256]{2,1,0:T(8,128)S(1)} %all_to_all.371, f32[]{:T(128)} %constant.46.clone.1), window={size=1x1x33 pad=0_0x0_0x16_16}, to_apply=%region_36.37 | reduce-window | flops 2097152 | bytes 524292 | tf_op jit(solution)/shard_map/reduce_window_max | solution.py:24
  (449 shorter events, 161.3 us)
Async XLA Ops:
  36.8 11.7 %copy-start.3 = (f32[8,32,256]{2,1,0:T(8,128)S(1)}, f32[8,32,256]{2,1,0:T(8,128)}, u32[]{:S(2)}) copy-start(f32[8,32,256]{2,1,0:T(8,128)} %param.3) | copy-start | bytes 786436
  38.5 44.3 %all-to-all-start.4 = ((f32[8,1,128]{2,1,0:T(1,128)}), f32[8,1,128]{2,1,0:T(1,128)S(1)}, u32[]{:S(2)}, u32[]{:S(2)}) async-start(f32[8,1,128]{2,1,0:T(1,128)} %reshape.110), calls=%async_computation.4 | async-start | bytes 8192 | tf_op jit(solution)/shard_map/all_to_all | solution.py:56
  82.8 26.8 %all-to-all-start.6 = ((f32[8,1,128]{2,1,0:T(1,128)}), f32[8,1,128]{2,1,0:T(1,128)S(1)}, u32[]{:S(2)}, u32[]{:S(2)}) async-start(f32[8,1,128]{2,1,0:T(1,128)} %reshape.112), calls=%async_computation.6 | async-start | bytes 8192 | tf_op jit(solution)/shard_map/all_to_all | solution.py:56
  130.0 14.8 %all-to-all-start.7 = ((f32[32,2,2,8]{3,2,1,0:T(2,128)}), f32[32,2,2,8]{3,2,1,0:T(2,128)S(1)}, u32[]{:S(2)}, u32[]{:S(2)}) async-start(f32[32,2,2,8]{3,2,1,0:T(2,128)} %constant_dynamic-update-slice_fusion.96), calls=%async_computation.7 | async-start | bytes 131072 | tf_op jit(solution)/shard_map/all_to_all | solution.py:59
  144.8 11.0 %all-to-all-start.5 = ((f32[32,2,2,8]{3,2,1,0:T(2,128)}), f32[32,2,2,8]{3,2,1,0:T(2,128)S(1)}, u32[]{:S(2)}, u32[]{:S(2)}) async-start(f32[32,2,2,8]{3,2,1,0:T(2,128)} %constant_dynamic-update-slice_fusion.64), calls=%async_computation.5 | async-start | bytes 131072 | tf_op jit(solution)/shard_map/all_to_all | solution.py:59
  163.4 11.0 %all-to-all-start.8 = ((f32[64,2,8]{2,1,0:T(2,128)}), f32[64,2,8]{2,1,0:T(2,128)S(1)}, u32[]{:S(2)}, u32[]{:S(2)}) async-start(f32[64,2,8]{2,1,0:T(2,128)} %log_add_fusion.10), calls=%async_computation.8 | async-start | bytes 131072 | tf_op jit(solution)/shard_map/all_to_all | solution.py:71
  176.2 17.8 %all-to-all-start.9 = ((f32[8,1,128]{2,1,0:T(1,128)}), f32[8,1,128]{2,1,0:T(1,128)S(1)}, u32[]{:S(2)}, u32[]{:S(2)}) async-start(f32[8,1,128]{2,1,0:T(1,128)} %reshape.114), calls=%async_computation.9 | async-start | bytes 8192 | tf_op jit(solution)/shard_map/all_to_all | solution.py:72
  227.9 11.0 %all-to-all-start.12 = ((f32[64,2,8]{2,1,0:T(2,128)}), f32[64,2,8]{2,1,0:T(2,128)S(1)}, u32[]{:S(2)}, u32[]{:S(2)}) async-start(f32[64,2,8]{2,1,0:T(2,128)} %log_add_fusion.7), calls=%async_computation.12 | async-start | bytes 131072 | tf_op jit(solution)/shard_map/all_to_all | solution.py:71
  238.9 13.7 %all-to-all-start.2 = ((f32[8,1,1024]{2,1,0:T(1,128)}), f32[8,1,1024]{2,1,0:T(1,128)S(1)}, u32[]{:S(2)}, u32[]{:S(2)}) async-start(f32[8,1,1024]{2,1,0:T(1,128)} %reshape.106), calls=%async_computation.2 | async-start | bytes 65536 | tf_op jit(solution)/shard_map/all_to_all | solution.py:56
  252.6 10.9 %all-to-all-start.13 = ((f32[8,1,128]{2,1,0:T(1,128)}), f32[8,1,128]{2,1,0:T(1,128)S(1)}, u32[]{:S(2)}, u32[]{:S(2)}) async-start(f32[8,1,128]{2,1,0:T(1,128)} %reshape.118), calls=%async_computation.13 | async-start | bytes 8192 | tf_op jit(solution)/shard_map/all_to_all | solution.py:72
  269.5 11.1 %all-to-all-start.14 = ((f32[8,1,1024]{2,1,0:T(1,128)}), f32[8,1,1024]{2,1,0:T(1,128)S(1)}, u32[]{:S(2)}, u32[]{:S(2)}) async-start(f32[8,1,1024]{2,1,0:T(1,128)} %reshape.120), calls=%async_computation.14 | async-start | bytes 65536 | tf_op jit(solution)/shard_map/all_to_all | solution.py:56
  280.6 11.2 %all-to-all-start.3 = ((f32[32,1,256]{2,1,0:T(1,128)}), f32[32,1,256]{2,1,0:T(1,128)S(1)}, u32[]{:S(2)}, u32[]{:S(2)}) async-start(f32[32,1,256]{2,1,0:T(1,128)} %reshape.108), calls=%async_computation.3 | async-start | bytes 65536 | tf_op jit(solution)/shard_map/all_to_all | solution.py:59
  291.7 14.3 %all-to-all-start.15 = ((f32[32,1,256]{2,1,0:T(1,128)}), f32[32,1,256]{2,1,0:T(1,128)S(1)}, u32[]{:S(2)}, u32[]{:S(2)}) async-start(f32[32,1,256]{2,1,0:T(1,128)} %reshape.122), calls=%async_computation.15 | async-start | bytes 65536 | tf_op jit(solution)/shard_map/all_to_all | solution.py:59
  356.5 21.2 %copy-start.2 = (f32[8,32,256]{2,1,0:T(8,128)S(1)}, f32[8,32,256]{2,1,0:T(8,128)}, u32[]{:S(2)}) copy-start(f32[8,32,256]{2,1,0:T(8,128)} %param.2) | copy-start | bytes 786436
  373.9 11.0 %all-to-all-start.19 = ((f32[32,1,256]{2,1,0:T(1,128)}), f32[32,1,256]{2,1,0:T(1,128)S(1)}, u32[]{:S(2)}, u32[]{:S(2)}) async-start(f32[32,1,256]{2,1,0:T(1,128)} %reshape.130), calls=%async_computation.19 | async-start | bytes 65536 | tf_op jit(solution)/shard_map/all_to_all | solution.py:59
  384.9 20.9 %all-to-all-start = ((f32[8,1,8192]{2,1,0:T(1,128)}), f32[8,1,8192]{2,1,0:T(1,128)S(1)}, u32[]{:S(2)}, u32[]{:S(2)}) async-start(f32[8,1,8192]{2,1,0:T(1,128)} %reshape.102), calls=%async_computation | async-start | bytes 524288 | tf_op jit(solution)/shard_map/all_to_all | solution.py:56
  405.9 11.0 %all-to-all-start.20 = ((f32[32,1,256]{2,1,0:T(1,128)}), f32[32,1,256]{2,1,0:T(1,128)S(1)}, u32[]{:S(2)}, u32[]{:S(2)}) async-start(f32[32,1,256]{2,1,0:T(1,128)} %reshape.132), calls=%async_computation.20 | async-start | bytes 65536 | tf_op jit(solution)/shard_map/all_to_all | solution.py:71
  422.9 15.7 %all-to-all-start.21 = ((f32[8,1,1024]{2,1,0:T(1,128)}), f32[8,1,1024]{2,1,0:T(1,128)S(1)}, u32[]{:S(2)}, u32[]{:S(2)}) async-start(f32[8,1,1024]{2,1,0:T(1,128)} %reshape.134), calls=%async_computation.21 | async-start | bytes 65536 | tf_op jit(solution)/shard_map/all_to_all | solution.py:72
  431.5 11.3 %copy-start = (f32[32,8,8,32]{3,2,1,0:T(8,128)}, f32[32,8,8,32]{3,2,1,0:T(8,128)S(1)}, u32[]{:S(2)}) copy-start(f32[32,8,8,32]{3,2,1,0:T(8,128)S(1)} %constant_dynamic-update-slice_fusion.3) | copy-start | bytes 786436
  456.2 6.7 copy-start.1
  458.8 14.3 %all-to-all-start.22 = ((f32[8,1,8192]{2,1,0:T(1,128)}), f32[8,1,8192]{2,1,0:T(1,128)S(1)}, u32[]{:S(2)}, u32[]{:S(2)}) async-start(f32[8,1,8192]{2,1,0:T(1,128)} %reshape.136), calls=%async_computation.22 | async-start | bytes 524288 | tf_op jit(solution)/shard_map/all_to_all | solution.py:56
  473.1 38.2 %all-to-all-start.1 = ((f32[32,1,2048]{2,1,0:T(1,128)}), f32[32,1,2048]{2,1,0:T(1,128)S(1)}, u32[]{:S(2)}, u32[]{:S(2)}) async-start(f32[32,1,2048]{2,1,0:T(1,128)} %reshape.104), calls=%async_computation.1 | async-start | bytes 524288 | tf_op jit(solution)/shard_map/all_to_all | solution.py:59
  511.3 15.9 %all-to-all-start.23 = ((f32[32,1,2048]{2,1,0:T(1,128)}), f32[32,1,2048]{2,1,0:T(1,128)S(1)}, u32[]{:S(2)}, u32[]{:S(2)}) async-start(f32[32,1,2048]{2,1,0:T(1,128)} %reshape.138), calls=%async_computation.23 | async-start | bytes 524288 | tf_op jit(solution)/shard_map/all_to_all | solution.py:59
  561.0 35.7 %all-to-all-start.24 = ((f32[32,1,2048]{2,1,0:T(1,128)}), f32[32,1,2048]{2,1,0:T(1,128)S(1)}, u32[]{:S(2)}, u32[]{:S(2)}) async-start(f32[32,1,2048]{2,1,0:T(1,128)} %reshape.140), calls=%async_computation.24 | async-start | bytes 524288 | tf_op jit(solution)/shard_map/all_to_all | solution.py:71
  596.7 15.7 %all-to-all-start.26 = ((f32[32,1,2048]{2,1,0:T(1,128)}), f32[32,1,2048]{2,1,0:T(1,128)S(1)}, u32[]{:S(2)}, u32[]{:S(2)}) async-start(f32[32,1,2048]{2,1,0:T(1,128)} %reshape.144), calls=%async_computation.26 | async-start | bytes 524288 | tf_op jit(solution)/shard_map/all_to_all | solution.py:71
  612.3 42.9 %all-to-all-start.25 = ((f32[8,1,8192]{2,1,0:T(1,128)}), f32[8,1,8192]{2,1,0:T(1,128)S(1)}, u32[]{:S(2)}, u32[]{:S(2)}) async-start(f32[8,1,8192]{2,1,0:T(1,128)} %reshape.142), calls=%async_computation.25 | async-start | bytes 524288 | tf_op jit(solution)/shard_map/all_to_all | solution.py:72
  655.3 17.3 %all-to-all-start.27 = ((f32[8,1,8192]{2,1,0:T(1,128)}), f32[8,1,8192]{2,1,0:T(1,128)S(1)}, u32[]{:S(2)}, u32[]{:S(2)}) async-start(f32[8,1,8192]{2,1,0:T(1,128)} %reshape.146), calls=%async_computation.27 | async-start | bytes 524288 | tf_op jit(solution)/shard_map/all_to_all | solution.py:72
